TPU v7x, 128 devices: a whole 4x4x4 slice. The times are simulated.
128 devices in a mesh: dp: 16 (over z, y), mp: 8 (over x, core).
Axes of the slice: x: 4, y: 4, z: 4, core: 2. Of those that a mesh axis runs over, the one named last changes fastest.
Arguments:
- cotangent: bfloat16 [32768, 4096], P('dp'), may hold values from -64 to 64, as said below
- activation: bfloat16 [32768, 8192], P('dp', 'mp'), may hold values from -64 to 64, as said below
Outputs:
- update: bfloat16 [4096, 8192], P('dp', 'mp')
Inputs may be any that keep to these rules, and one draw needn't show every extreme that they name: `cotangent`: real-valued entries. `activation`: real-valued entries.
All inputs are finite; a program needn't handle non-finite values.
Results may differ from a plain program's by a relative error of at most 0.0054.
Values may be sent and summed in bfloat16 or wider, within the bound.
A program may use at most 256 MiB of HBM per device.

v0:
```python
import math
import jax
import jax.numpy as jnp
from jax import lax
from jax.sharding import PartitionSpec as P

N = 8192
ROWS = 4096
LINEAR_COEF = 3.4445
CUBIC_COEF = -4.775
QUINTIC_COEF = 2.0315
NORM_EPSILON = 1e-07
NORM_SHARE = 0.25
CONTRACT_FIRST = (((0,), (0,)), ((), ()))
CONTRACT_LAST = (((1,), (1,)), ((), ()))


def local(cotangent, activation):
    section = cotangent
    gradient = lax.psum_scatter(
        lax.dot_general(section, activation, CONTRACT_FIRST, preferred_element_type=jnp.float32),
        "dp",
        scatter_dimension=0,
        tiled=True,
    )
    sum_squares = lax.psum(jnp.sum(gradient * gradient), ("dp", "mp"))
    factor = NORM_SHARE * math.sqrt(ROWS) / (jnp.sqrt(sum_squares) + NORM_EPSILON)
    normalized = (gradient * factor).astype(jnp.bfloat16)
    weight_column = lax.all_gather(normalized, "dp", axis=0, tiled=True)
    section = weight_column
    gram_tile = lax.psum_scatter(
        lax.dot_general(section, normalized, CONTRACT_LAST, preferred_element_type=jnp.float32),
        "mp",
        scatter_dimension=0,
        tiled=True,
    ).T.astype(jnp.bfloat16)
    row_panel = lax.all_gather(gram_tile, "mp", axis=1, tiled=True)
    section = row_panel
    square_tile = jnp.dot(
        section,
        lax.all_gather(gram_tile, "dp", axis=0, tiled=True),
        preferred_element_type=jnp.float32,
    )
    polynomial = (CUBIC_COEF * gram_tile.astype(jnp.float32) + QUINTIC_COEF * square_tile).astype(
        jnp.bfloat16
    )
    section = weight_column
    product_tile = jnp.dot(
        lax.all_gather(polynomial, "mp", axis=1, tiled=True),
        section,
        preferred_element_type=jnp.float32,
    )
    rescale = math.sqrt(N)
    return (rescale * (LINEAR_COEF * normalized.astype(jnp.float32) + product_tile)).astype(
        jnp.bfloat16
    )


def solution(mesh):
    return jax.shard_map(
        local,
        mesh=mesh,
        in_specs=(P("dp", None), P("dp", "mp")),
        out_specs=P("dp", "mp"),
        check_vma=False,
    )
```

profile of v0, /device:TPU:1, one launch (start us, length us, event | category | flops | bytes accessed | tf_op | source)
XLA Modules:
  0.0 457.3 jit_solution(6413023268243869418)
XLA Ops:
  6.5 23.7 %fusion.4 = f32[4096,1024]{1,0:T(8,128)} fusion(bf16[2048,4096]{1,0:T(8,128)(2,1)} %param.2, bf16[2048,1024]{1,0:T(8,128)(2,1)} %param.3), kind=kOutput, calls=%fused_computation.9 | convolution fusion | flops 17179869184 | bytes 37748736 | tf_op jit(solution)/shard_map/dot_general | solution.py:21
  30.3 0.0 reduce-scatter.3.cloned.1.call-update
  30.3 0.0 all-gather.5.cloned.1.call-start
  30.3 113.7 %reduce-scatter.3.cloned.1.call-done = f32[256,1024]{1,0:T(8,128)} async-done(((f32[4096,1024]{1,0:T(8,128)}), f32[256,1024]{1,0:T(8,128)}) %reduce-scatter.3.cloned.1.call-update) | async-done | bytes 1048592 | tf_op jit(solution)/shard_map/reduce_scatter | solution.py:20
  144.0 2.1 multiply_reduce_fusion
  146.1 64.8 %psum.7 = f32[]{:T(128)} all-reduce(f32[]{:T(128)} %multiply_reduce_fusion), channel_id=1, replica_groups=mesh['dp'=16,'mp'=8] {'dp','mp'}, use_global_device_ids=true, to_apply=%region_2.0 | all-reduce | flops 1 | bytes 8 | tf_op jit(solution)/shard_map/psum | solution.py:26
  211.6 2.1 multiply_convert_fusion
  213.7 0.0 all-gather.5.cloned.1.call-update
  213.7 0.0 reduce-scatter.5.cloned.1.call-start
  213.8 68.2 %all-gather.5.cloned.1.call-done = bf16[4096,1024]{1,0:T(8,128)(2,1)} async-done(((bf16[256,1024]{1,0:T(8,128)(2,1)}), bf16[4096,1024]{1,0:T(8,128)(2,1)}) %all-gather.5.cloned.1.call-update) | async-done | bytes 8388624 | tf_op jit(solution)/shard_map/all_gather | solution.py:29
  282.0 7.8 %fusion.5 = f32[4096,256]{1,0:T(8,128)} fusion(bf16[4096,1024]{1,0:T(8,128)(2,1)} %all-gather.5.cloned.1.call-done, bf16[256,1024]{1,0:T(8,128)(2,1)} %multiply_convert_fusion), kind=kOutput, calls=%fused_computation.10 | convolution fusion | flops 2147483648 | bytes 13107200 | tf_op jit(solution)/shard_map/dot_general | solution.py:32
  289.8 0.0 reduce-scatter.5.cloned.1.call-update
  289.8 0.0 all-gather.7.cloned.1.call-start
  289.9 34.7 %reduce-scatter.5.cloned.1.call-done = f32[512,256]{1,0:T(8,128)} async-done(((f32[4096,256]{1,0:T(8,128)}), f32[512,256]{1,0:T(8,128)}) %reduce-scatter.5.cloned.1.call-update) | async-done | bytes 524304 | tf_op jit(solution)/shard_map/reduce_scatter | solution.py:31
  324.5 1.8 convert_bitcast_fusion
  326.3 0.0 all-gather.9.cloned.1.call-start
  326.4 0.5 all-gather.9.cloned.1.call-update
  326.9 0.0 all-gather.11.cloned.1.call-start
  327.0 26.9 %all-gather.7.cloned.1.call-done = bf16[256,4096]{0,1:T(8,128)(2,1)} async-done(((bf16[256,512]{0,1:T(8,128)(2,1)}), bf16[256,4096]{0,1:T(8,128)(2,1)}) %all-gather.7.cloned.1.call-update) | async-done | bytes 2097168 | tf_op jit(solution)/shard_map/all_gather | solution.py:37
  353.9 58.8 %all-gather.9.cloned.1.call-done = bf16[4096,512]{0,1:T(8,128)(2,1)} async-done(((bf16[256,512]{0,1:T(8,128)(2,1)}), bf16[4096,512]{0,1:T(8,128)(2,1)}) %all-gather.9.cloned.1.call-update) | async-done | bytes 4194320 | tf_op jit(solution)/shard_map/all_gather | solution.py:41
  412.6 4.8 %fusion.3 = bf16[256,512]{0,1:T(8,128)(2,1)} fusion(bf16[4096,512]{0,1:T(8,128)(2,1)} %all-gather.9.cloned.1.call-done, bf16[256,4096]{0,1:T(8,128)(2,1)} %all-gather.7.cloned.1.call-done, bf16[256,512]{0,1:T(8,128)(2,1)} %convert_bitcast_fusion), kind=kOutput, calls=%fused_computation.5 | convolution fusion | flops 1074397184 | bytes 6815744 | tf_op jit(solution)/shard_map/dot_general | solution.py:39
  417.4 0.0 all-gather.11.cloned.1.call-update
  417.5 25.8 %all-gather.11.cloned.1.call-done = bf16[256,4096]{0,1:T(8,128)(2,1)} async-done(((bf16[256,512]{0,1:T(8,128)(2,1)}), bf16[256,4096]{0,1:T(8,128)(2,1)}) %all-gather.11.cloned.1.call-update) | async-done | bytes 2097168 | tf_op jit(solution)/shard_map/all_gather | solution.py:49
  443.3 7.2 %fusion.1 = bf16[256,1024]{1,0:T(8,128)(2,1)} fusion(bf16[256,4096]{0,1:T(8,128)(2,1)} %all-gather.11.cloned.1.call-done, bf16[4096,1024]{1,0:T(8,128)(2,1)} %all-gather.5.cloned.1.call-done, bf16[256,1024]{1,0:T(8,128)(2,1)S(1)} %copy-done), kind=kOutput, calls=%fused_computation.2 | convolution fusion | flops 2148794368 | bytes 11534336 | tf_op jit(solution)/shard_map/dot_general | solution.py:48
  (4 shorter events, 0.0 us)
Async XLA Ops:
  6.5 137.5 %reduce-scatter.3.cloned.1.call-start = ((), (), s32[]{:S(2)}) async-start(), calls=%async_computation.2 | async-start | bytes 17825792 | tf_op jit(solution)/shard_map/reduce_scatter | solution.py:20
  30.3 251.7 %all-gather.5.cloned.1.call-start = ((), (), s32[]{:S(2)}) async-start(), calls=%async_computation.3 | async-start | bytes 8912896 | tf_op jit(solution)/shard_map/all_gather | solution.py:29
  213.7 110.8 %reduce-scatter.5.cloned.1.call-start = ((), (), s32[]{:S(2)}) async-start(), calls=%async_computation.4 | async-start | bytes 4718592 | tf_op jit(solution)/shard_map/reduce_scatter | solution.py:31
  289.8 64.1 %all-gather.7.cloned.1.call-start = ((), (), s32[]{:S(2)}) async-start(), calls=%async_computation.5 | async-start | bytes 2359296 | tf_op jit(solution)/shard_map/all_gather | solution.py:37
  326.3 86.3 %all-gather.9.cloned.1.call-start = ((), (), s32[]{:S(2)}) async-start(), calls=%async_computation.6 | async-start | bytes 4456448 | tf_op jit(solution)/shard_map/all_gather | solution.py:41
  326.9 116.3 %copy-start = (bf16[256,1024]{1,0:T(8,128)(2,1)S(1)}, bf16[256,1024]{1,0:T(8,128)(2,1)}, u32[]{:S(2)}) copy-start(bf16[256,1024]{1,0:T(8,128)(2,1)} %multiply_convert_fusion) | copy-start | bytes 1572868
  326.9 116.3 %all-gather.11.cloned.1.call-start = ((), (), s32[]{:S(2)}) async-start(), calls=%async_computation.7 | async-start | bytes 2359296 | tf_op jit(solution)/shard_map/all_gather | solution.py:49
Sparse Core Ops, SparseCore 0:
  30.4 113.5 reduce-scatter.2
  213.9 68.1 all-gather.4
  289.9 34.5 reduce-scatter.4
  326.5 27.3 all-gather.6
  355.8 56.7 all-gather.8
  417.6 25.6 all-gather.10
where the time goes:
time: 458 us; the launch traced here: 457 us
  waiting for transfers between devices  329 us (72%)
  blocking collectives  64.8 us (14%)
  matrix products  43.5 us (9%)
  between operations  14.2 us (3%)
  other arithmetic  6 us (1%)
    reduce_scatter x1, waiting for transfers between devices, local(): lax.psum_scatter(lax.dot_general(section, activation, CONTRACT_FIRST, pre...  114 us
    all_gather x1, waiting for transfers between devices, local(): weight_column = lax.all_gather(normalized, 'dp', axis=0, tiled=True)  68.2 us
    psum x1, blocking collectives, local(): sum_squares = lax.psum(jnp.sum(gradient * gradient), ('dp', 'mp'))  64.8 us
    all_gather x1, waiting for transfers between devices, local(): lax.all_gather(gram_tile, 'dp', axis=0, tiled=True)  58.8 us
    reduce_scatter x1, waiting for transfers between devices, local(): lax.psum_scatter(lax.dot_general(section, normalized, CONTRACT_LAST, pref...  34.7 us
    all_gather x1, waiting for transfers between devices, local(): row_panel = lax.all_gather(gram_tile, 'mp', axis=1, tiled=True)  26.9 us
    all_gather x1, waiting for transfers between devices, local(): lax.all_gather(polynomial, 'mp', axis=1, tiled=True)  25.8 us
    dot_general x1, matrix products, local(): lax.dot_general(section, activation, CONTRACT_FIRST, preferred_element_ty...  23.7 us
  transfers between devices with their start and end apart: 6, of which 6 were waited for; matrix products, arithmetic and copies ran while one was open for 0% of the time, Pallas kernels for 0%

commit v1 on v0

--- a/solution.py
+++ b/solution.py
@@ -34,7 +34,9 @@
         scatter_dimension=0,
         tiled=True,
     ).T.astype(jnp.bfloat16)
-    row_panel = lax.all_gather(gram_tile, "mp", axis=1, tiled=True)
+    row_panel = jnp.concatenate(
+        lax.all_to_all(jnp.stack([gram_tile] * lax.axis_size("mp")), "mp", 0, 0), axis=1
+    )
     section = row_panel
     square_tile = jnp.dot(
         section,

time: 458 us -> 429 us (0.937)
  waiting for transfers between devices: 329 us -> 268 us
  blocking collectives: 64.8 us -> 97.3 us
    all_gather x1, waiting for transfers between devices: 58.8 us -> 25.2 us  [local(): lax.all_gather(gram_tile, 'dp', axis=0, tiled=True)]
    all_to_all x0 -> x1, blocking collectives: none -> 32.5 us  [local(): lax.all_to_all(jnp.stack([gram_tile] * lax.axis_size('mp')), 'mp', 0, 0)]
    all_gather x1 -> x0, waiting for transfers between devices: 26.9 us -> none  [local(): row_panel = lax.all_gather(gram_tile, 'mp', axis=1, tiled=True)]
  transfers between devices with their start and end apart: 6 -> 5, of which waited for: 6 -> 5; matrix products, arithmetic and copies ran while one was open for 0% -> 0% of each run, Pallas kernels for 0% -> 0%
where the time goes in v1:
time: 429 us
  waiting for transfers between devices  268 us (62%)
  blocking collectives  97.3 us (23%)
  matrix products  42.9 us (10%)
  between operations  13.9 us (3%)
  other arithmetic  6 us (1%)
    reduce_scatter x1, waiting for transfers between devices, local(): lax.psum_scatter(lax.dot_general(section, activation, CONTRACT_FIRST, pre...  114 us
    all_gather x1, waiting for transfers between devices, local(): weight_column = lax.all_gather(normalized, 'dp', axis=0, tiled=True)  68.2 us
    psum x1, blocking collectives, local(): sum_squares = lax.psum(jnp.sum(gradient * gradient), ('dp', 'mp'))  64.7 us
    reduce_scatter x1, waiting for transfers between devices, local(): lax.psum_scatter(lax.dot_general(section, normalized, CONTRACT_LAST, pref...  34.7 us
    all_to_all x1, blocking collectives, local(): lax.all_to_all(jnp.stack([gram_tile] * lax.axis_size('mp')), 'mp', 0, 0)  32.5 us
    all_gather x1, waiting for transfers between devices, local(): lax.all_gather(polynomial, 'mp', axis=1, tiled=True)  25.8 us
    all_gather x1, waiting for transfers between devices, local(): lax.all_gather(gram_tile, 'dp', axis=0, tiled=True)  25.2 us
    dot_general x1, matrix products, local(): lax.dot_general(section, activation, CONTRACT_FIRST, preferred_element_ty...  23.7 us
  transfers between devices with their start and end apart: 5, of which 5 were waited for; matrix products, arithmetic and copies ran while one was open for 0% of the time, Pallas kernels for 0%

profile of v1, /device:TPU:1, one launch (start us, length us, event | category | flops | bytes accessed | tf_op | source)
XLA Modules:
  0.0 428.9 jit_solution(605442620685837979)
XLA Ops:
  6.5 23.7 %fusion.4 = f32[4096,1024]{1,0:T(8,128)} fusion(bf16[2048,4096]{1,0:T(8,128)(2,1)} %param.2, bf16[2048,1024]{1,0:T(8,128)(2,1)} %param.3), kind=kOutput, calls=%fused_computation.9 | convolution fusion | flops 17179869184 | bytes 37748736 | tf_op jit(solution)/shard_map/dot_general | solution.py:21
  30.3 0.0 reduce-scatter.3.cloned.1.call-update
  30.3 0.0 all-gather.4.cloned.1.call-start
  30.4 113.7 %reduce-scatter.3.cloned.1.call-done = f32[256,1024]{1,0:T(8,128)} async-done(((f32[4096,1024]{1,0:T(8,128)}), f32[256,1024]{1,0:T(8,128)}) %reduce-scatter.3.cloned.1.call-update) | async-done | bytes 1048592 | tf_op jit(solution)/shard_map/reduce_scatter | solution.py:20
  144.0 2.1 multiply_reduce_fusion
  146.1 64.7 %psum.7 = f32[]{:T(128)} all-reduce(f32[]{:T(128)} %multiply_reduce_fusion), channel_id=1, replica_groups=mesh['dp'=16,'mp'=8] {'dp','mp'}, use_global_device_ids=true, to_apply=%region_2.0 | all-reduce | flops 1 | bytes 8 | tf_op jit(solution)/shard_map/psum | solution.py:26
  211.6 2.1 multiply_convert_fusion
  213.7 0.0 all-gather.4.cloned.1.call-update
  213.7 0.0 reduce-scatter.5.cloned.1.call-start
  213.8 68.2 %all-gather.4.cloned.1.call-done = bf16[4096,1024]{1,0:T(8,128)(2,1)} async-done(((bf16[256,1024]{1,0:T(8,128)(2,1)}), bf16[4096,1024]{1,0:T(8,128)(2,1)}) %all-gather.4.cloned.1.call-update) | async-done | bytes 8388624 | tf_op jit(solution)/shard_map/all_gather | solution.py:29
  282.0 7.8 %fusion.5 = f32[4096,256]{1,0:T(8,128)} fusion(bf16[4096,1024]{1,0:T(8,128)(2,1)} %all-gather.4.cloned.1.call-done, bf16[256,1024]{1,0:T(8,128)(2,1)} %multiply_convert_fusion), kind=kOutput, calls=%fused_computation.10 | convolution fusion | flops 2147483648 | bytes 13107200 | tf_op jit(solution)/shard_map/dot_general | solution.py:32
  289.8 0.0 reduce-scatter.5.cloned.1.call-update
  289.8 0.0 all-gather.6.cloned.1.call-start
  289.9 34.7 %reduce-scatter.5.cloned.1.call-done = f32[512,256]{1,0:T(8,128)} async-done(((f32[4096,256]{1,0:T(8,128)}), f32[512,256]{1,0:T(8,128)}) %reduce-scatter.5.cloned.1.call-update) | async-done | bytes 524304 | tf_op jit(solution)/shard_map/reduce_scatter | solution.py:31
  324.5 1.8 convert_bitcast_fusion
  326.3 0.0 all-gather.6.cloned.1.call-update
  326.3 0.0 all-gather.8.cloned.1.call-start
  326.4 1.1 stack.2
  327.5 32.5 %all_to_all.5 = bf16[8,256,512]{1,2,0:T(8,128)(2,1)S(1)} all-to-all(bf16[8,256,512]{1,2,0:T(8,128)(2,1)S(1)} %stack.2), channel_id=1, replica_groups=mesh['dp'=16,'mp'=8] {'mp'}, dimensions={0} | all-to-all | bytes 4194304 | tf_op jit(solution)/shard_map/all_to_all | solution.py:38
  360.0 25.2 %all-gather.6.cloned.1.call-done = bf16[4096,512]{0,1:T(8,128)(2,1)} async-done(((bf16[256,512]{0,1:T(8,128)(2,1)}), bf16[4096,512]{0,1:T(8,128)(2,1)}) %all-gather.6.cloned.1.call-update) | async-done | bytes 4194320 | tf_op jit(solution)/shard_map/all_gather | solution.py:43
  385.2 4.2 fusion.3
  389.4 0.0 all-gather.8.cloned.1.call-update
  389.4 25.8 %all-gather.8.cloned.1.call-done = bf16[256,4096]{0,1:T(8,128)(2,1)} async-done(((bf16[256,512]{0,1:T(8,128)(2,1)}), bf16[256,4096]{0,1:T(8,128)(2,1)}) %all-gather.8.cloned.1.call-update) | async-done | bytes 2097168 | tf_op jit(solution)/shard_map/all_gather | solution.py:51
  415.2 7.2 %fusion.1 = bf16[256,1024]{1,0:T(8,128)(2,1)} fusion(bf16[256,4096]{0,1:T(8,128)(2,1)} %all-gather.8.cloned.1.call-done, bf16[4096,1024]{1,0:T(8,128)(2,1)} %all-gather.4.cloned.1.call-done, bf16[256,1024]{1,0:T(8,128)(2,1)S(1)} %copy-done), kind=kOutput, calls=%fused_computation.2 | convolution fusion | flops 2148794368 | bytes 11534336 | tf_op jit(solution)/shard_map/dot_general | solution.py:50
  (5 shorter events, 0.0 us)
Async XLA Ops:
  6.5 137.5 %reduce-scatter.3.cloned.1.call-start = ((), (), s32[]{:S(2)}) async-start(), calls=%async_computation.3 | async-start | bytes 17825792 | tf_op jit(solution)/shard_map/reduce_scatter | solution.py:20
  30.3 251.7 %all-gather.4.cloned.1.call-start = ((), (), s32[]{:S(2)}) async-start(), calls=%async_computation.4 | async-start | bytes 8912896 | tf_op jit(solution)/shard_map/all_gather | solution.py:29
  213.7 110.8 %reduce-scatter.5.cloned.1.call-start = ((), (), s32[]{:S(2)}) async-start(), calls=%async_computation.5 | async-start | bytes 4718592 | tf_op jit(solution)/shard_map/reduce_scatter | solution.py:31
  289.8 95.4 %all-gather.6.cloned.1.call-start = ((), (), s32[]{:S(2)}) async-start(), calls=%async_computation.6 | async-start | bytes 4456448 | tf_op jit(solution)/shard_map/all_gather | solution.py:43
  326.3 58.9 %copy-start.1 = (bf16[256,512]{0,1:T(8,128)(2,1)S(1)}, bf16[256,512]{0,1:T(8,128)(2,1)}, u32[]{:S(2)}) copy-start(bf16[256,512]{0,1:T(8,128)(2,1)} %convert_bitcast_fusion) | copy-start | bytes 786436
  326.3 88.9 %all-gather.8.cloned.1.call-start = ((), (), s32[]{:S(2)}) async-start(), calls=%async_computation.7 | async-start | bytes 2359296 | tf_op jit(solution)/shard_map/all_gather | solution.py:51
  385.2 30.0 %copy-start = (bf16[256,1024]{1,0:T(8,128)(2,1)S(1)}, bf16[256,1024]{1,0:T(8,128)(2,1)}, u32[]{:S(2)}) copy-start(bf16[256,1024]{1,0:T(8,128)(2,1)} %multiply_convert_fusion) | copy-start | bytes 1572868
Sparse Core Ops, SparseCore 0:
  30.4 113.5 reduce-scatter.2
  213.9 68.1 all-gather.3
  289.9 34.5 reduce-scatter.4
  326.5 58.6 all-gather.5
  389.5 25.6 all-gather.7
